TPU v7x, 32 devices: a whole 2x2x4 slice. The times are simulated.
32 devices in a mesh: row: 4 (over y, core), col: 8 (over z, x).
Axes of the slice: x: 2, y: 2, z: 4, core: 2. Of those that a mesh axis runs over, the one named last changes fastest.
Arguments:
- calib: bfloat16 [256, 8192], replicated, may hold values from -6 to 6
- gate_a: bfloat16 [8192, 28672], P('col', 'row'), may hold values from -0.0625 to 0.0625
- up_a: bfloat16 [8192, 28672], P('col', 'row'), may hold values from -0.0625 to 0.0625
- gate_b: bfloat16 [8192, 28672], P('row', 'col'), may hold values from -0.0625 to 0.0625
- up_b: bfloat16 [8192, 28672], P('row', 'col'), may hold values from -0.0625 to 0.0625
- down_a: bfloat16 [28672, 1024], P(('row', 'col')), may hold values from -6 to 6
- down_b: bfloat16 [28672, 1024], P('col', 'row'), may hold values from -6 to 6
Outputs:
- joined: bfloat16 [28672, 1024], P(('row', 'col'))
All inputs are finite; a program needn't handle non-finite values.
Results may differ from a plain program's by a relative error of at most 0.025.
Values may be sent and summed in bfloat16 or wider, within the bound.
A program may use at most 384 MiB of HBM per device.

v0:
```python
import jax
import jax.numpy as jnp
from jax import lax
from jax.experimental import pallas as pl
from jax.experimental.pallas import tpu as pltpu
from jax.sharding import PartitionSpec as P

ITERS = 3


softness = 0.02
statistic_floor = 1e-05
LANES = 128


def standardize(gate_pre, up_preactivation):
    hidden = jax.nn.silu(gate_pre) * up_preactivation
    center = jnp.mean(hidden, axis=0, keepdims=True)
    spread = jnp.mean(jnp.square(hidden - center), axis=0, keepdims=True)
    return ((hidden - center) * lax.rsqrt(spread + statistic_floor)).astype(jnp.bfloat16)


def block_of(size, most):
    block = most
    while size % block:
        block //= 2
    return block


def lane_chunk(size, most):
    chunk = most
    while size % chunk:
        chunk -= LANES
    return chunk


def make_kernel(scores_a, scores_b, multiplier):
    rows, depth = scores_a.shape
    cols = scores_b.shape[0]
    block = block_of(rows, 512)
    chunk = lane_chunk(cols, 512)

    def body(a_ref, b_ref, k_ref, s_ref):
        total = jnp.zeros((block, LANES), jnp.float32)
        for start in range(0, cols, chunk):
            logits = lax.dot_general(
                a_ref[...], b_ref[start : start + chunk, :], (((1,), (1,)), ((), ())),
                preferred_element_type=jnp.float32,
            )
            values = jnp.exp(logits * multiplier)
            k_ref[:, start : start + chunk] = values.astype(jnp.bfloat16)
            for lane in range(0, chunk, LANES):
                total = total + values[:, lane : lane + LANES]
        s_ref[...] = jnp.sum(total, axis=1, keepdims=True)

    return pl.pallas_call(
        body,
        grid=(rows // block,),
        in_specs=[
            pl.BlockSpec((block, depth), lambda i: (i, 0)),
            pl.BlockSpec((cols, depth), lambda i: (0, 0)),
        ],
        out_specs=[
            pl.BlockSpec((block, cols), lambda i: (i, 0)),
            pl.BlockSpec((block, 1), lambda i: (i, 0)),
        ],
        out_shape=[
            jax.ShapeDtypeStruct((rows, cols), jnp.bfloat16),
            jax.ShapeDtypeStruct((rows, 1), jnp.float32),
        ],
        cost_estimate=pl.CostEstimate(
            flops=2 * rows * cols * depth, bytes_accessed=2 * rows * cols, transcendentals=rows * cols
        ),
        name="make_kernel",
    )(scores_a, scores_b)


def row_pass(kernel, column_scaling):
    rows, cols = kernel.shape
    block = block_of(rows, 512)
    group = block_of(block, 64)

    def body(k_ref, c_ref, s_ref):
        @pl.loop(0, block // group)
        def _(step):
            base = pl.multiple_of(step * group, group)
            total = jnp.zeros((group, LANES), jnp.float32)
            for lane in range(0, cols, LANES):
                total = total + (
                    k_ref[pl.ds(base, group), lane : lane + LANES].astype(jnp.float32)
                    * c_ref[:, lane : lane + LANES]
                )
            s_ref[pl.ds(base, group), :] = jnp.sum(total, axis=1, keepdims=True)

    return pl.pallas_call(
        body,
        grid=(rows // block,),
        in_specs=[
            pl.BlockSpec((block, cols), lambda i: (i, 0)),
            pl.BlockSpec((1, cols), lambda i: (0, 0)),
        ],
        out_specs=pl.BlockSpec((block, 1), lambda i: (i, 0)),
        out_shape=jax.ShapeDtypeStruct((rows, 1), jnp.float32),
        cost_estimate=pl.CostEstimate(
            flops=2 * rows * cols, bytes_accessed=2 * rows * cols, transcendentals=0
        ),
        name="row_pass",
    )(kernel, column_scaling)


def col_pass(kernel, row_scale):
    rows, cols = kernel.shape
    block = block_of(rows, 512)

    def body(k_ref, r_ref, s_ref):
        @pl.when(pl.program_id(0) == 0)
        def _():
            s_ref[...] = jnp.zeros_like(s_ref)

        for lane in range(0, cols, LANES):
            part = k_ref[:, lane : lane + LANES].astype(jnp.float32) * r_ref[...]
            s_ref[:, lane : lane + LANES] += jnp.sum(part, axis=0, keepdims=True)

    return pl.pallas_call(
        body,
        grid=(rows // block,),
        in_specs=[
            pl.BlockSpec((block, cols), lambda i: (i, 0)),
            pl.BlockSpec((block, LANES), lambda i: (i, 0)),
        ],
        out_specs=pl.BlockSpec((1, cols), lambda i: (0, 0)),
        out_shape=jax.ShapeDtypeStruct((1, cols), jnp.float32),
        cost_estimate=pl.CostEstimate(
            flops=2 * rows * cols, bytes_accessed=2 * rows * cols, transcendentals=0
        ),
        name="col_pass",
    )(kernel, jnp.broadcast_to(row_scale, (rows, LANES)))


def scores_of(gate_pre, up_pre, axis, parts, wire):
    tokens, width = gate_pre.shape
    own = width // parts
    both = jnp.stack((gate_pre.astype(wire), up_pre.astype(wire)))
    both = both.reshape(2, tokens, parts, own).transpose(2, 0, 1, 3)
    summed = lax.psum_scatter(both, axis, scatter_dimension=0, tiled=False).astype(jnp.float32)
    mine = standardize(summed[0], summed[1]).T
    return lax.all_gather(mine, axis, axis=0, tiled=True)


def solution(mesh):
    n_row, n_col = mesh.shape["row"], mesh.shape["col"]

    def per_device(calib, gate_a, up_a, gate_b, up_b, down_a, down_b):
        width_a = gate_a.shape[0]
        width_b = gate_b.shape[0]
        inputs_a = lax.dynamic_slice_in_dim(calib, lax.axis_index("col") * width_a, width_a, 1)
        inputs_b = lax.dynamic_slice_in_dim(calib, lax.axis_index("row") * width_b, width_b, 1)
        gate_pre_a = jnp.dot(inputs_a, gate_a, preferred_element_type=jnp.float32)
        up_pre_a = jnp.dot(inputs_a, up_a, preferred_element_type=jnp.float32)
        gate_pre_b = jnp.dot(inputs_b, gate_b, preferred_element_type=jnp.float32)
        up_pre_b = jnp.dot(inputs_b, up_b, preferred_element_type=jnp.float32)
        scores_a = scores_of(gate_pre_a, up_pre_a, "col", n_col, jnp.bfloat16)
        scores_b = scores_of(gate_pre_b, up_pre_b, "row", n_row, jnp.float32)
        rows_full = lax.all_gather(down_b, "row", axis=1, tiled=True)
        multiplier = 1.0 / (calib.shape[0] * softness)
        kernel, row_part = make_kernel(scores_a, scores_b, multiplier)
        for step in range(ITERS):
            if step:
                row_part = row_pass(kernel, column_scaling)
            row_scale = 1.0 / lax.psum(row_part[:, 0], "col")[:, None]
            column_scaling = 1.0 / lax.psum(col_pass(kernel, row_scale), "row")
        scaled = (rows_full.astype(jnp.float32) * column_scaling.reshape(-1, 1)).astype(jnp.bfloat16)
        window = scaled.shape[1]
        pieces = []
        for cut in range(0, window, window // 4):
            part = jnp.dot(kernel, scaled[:, cut : cut + window // 4], preferred_element_type=jnp.float32)
            part = (part * row_scale).astype(jnp.bfloat16)
            pieces.append(lax.psum_scatter(part, "col", scatter_dimension=0, tiled=True))
        aligned = jnp.concatenate(pieces, axis=1).astype(jnp.float32)
        return ((down_a.astype(jnp.float32) + aligned) * 0.5).astype(jnp.bfloat16)

    placed = (
        P(),
        P("col", "row"),
        P("col", "row"),
        P("row", "col"),
        P("row", "col"),
        P(("row", "col"), None),
        P("col", "row"),
    )
    return jax.shard_map(
        per_device, mesh=mesh, in_specs=placed, out_specs=P(("row", "col"), None), check_vma=False
    )
```

profile of v0, /device:TPU:0, one launch (start us, length us, event | category | flops | bytes accessed | tf_op | source)
XLA Modules:
  0.0 1022.6 jit_solution(7075433411296789035)
XLA Ops:
  6.5 11.1 %convolution_convert_fusion.1 = bf16[256,7168]{1,0:T(8,128)(2,1)} fusion(bf16[1024,7168]{1,0:T(8,128)(2,1)} %param.8, bf16[256,8192]{1,0:T(8,128)(2,1)} %param.7, s32[]{:T(128)S(6)} %select_n.6), kind=kOutput, calls=%fused_computation.10 | convolution fusion | flops 3759931392 | bytes 18874372 | tf_op jit(solution)/shard_map/dot_general | solution.py:158
  17.7 5.9 copy.12
  23.6 11.1 %convolution_convert_fusion = bf16[256,7168]{1,0:T(8,128)(2,1)} fusion(bf16[1024,7168]{1,0:T(8,128)(2,1)} %param.9, bf16[256,8192]{1,0:T(8,128)(2,1)} %param.7, s32[]{:T(128)S(6)} %select_n.6), kind=kOutput, calls=%fused_computation.9 | convolution fusion | flops 3759931392 | bytes 18874372 | tf_op jit(solution)/shard_map/dot_general | solution.py:159
  34.7 5.9 copy.13
  40.6 6.8 maximum_bitcast_fusion
  48.0 9.6 fusion.10
  57.5 13.2 %fusion.8 = f32[256,3584]{0,1:T(8,128)} fusion(bf16[2048,3584]{1,0:T(8,128)(2,1)} %param.11, bf16[256,8192]{1,0:T(8,128)(2,1)} %param.7, s32[]{:T(128)S(6)} %select_n.7), kind=kOutput, calls=%fused_computation.18 | convolution fusion | flops 3758096384 | bytes 19398660 | tf_op jit(solution)/shard_map/dot_general | solution.py:161
  70.7 5.6 maximum_bitcast_fusion.1
  76.4 106.8 %reduce-scatter.7.cloned.1.call-done = bf16[1,2,256,896]{2,3,1,0:T(8,128)(2,1)} async-done(((bf16[8,2,256,896]{2,3,1,0:T(8,128)(2,1)}), bf16[1,2,256,896]{2,3,1,0:T(8,128)(2,1)}) %reduce-scatter.7.cloned.1.call-update) | async-done | bytes 917520 | tf_op jit(solution)/shard_map/reduce_scatter | solution.py:145
  184.5 66.3 %reduce-scatter.9.cloned.1.call-done = f32[1,2,256,896]{2,3,1,0:T(8,128)} async-done(((f32[4,2,256,896]{2,3,1,0:T(8,128)}), f32[1,2,256,896]{2,3,1,0:T(8,128)}) %reduce-scatter.9.cloned.1.call-update) | async-done | bytes 1835024 | tf_op jit(solution)/shard_map/reduce_scatter | solution.py:145
  256.6 18.9 %all-gather.6.cloned.1.call-done.b_ref = bf16[3584,256]{1,0:T(8,128)(2,1)} async-done(((bf16[896,256]{1,0:T(8,128)(2,1)}), bf16[3584,256]{1,0:T(8,128)(2,1)}) %all-gather.6.cloned.1.call-update) | async-done | bytes 1835024 | tf_op jit(solution)/shard_map/all_gather | solution.py:147
  275.5 68.3 %all-gather.4.cloned.1.call-done.a_ref = bf16[7168,256]{1,0:T(8,128)(2,1)} async-done(((bf16[896,256]{1,0:T(8,128)(2,1)}), bf16[7168,256]{1,0:T(8,128)(2,1)}) %all-gather.4.cloned.1.call-update) | async-done | bytes 3670032 | tf_op jit(solution)/shard_map/all_gather | solution.py:147
  343.8 26.4 %make_kernel.1 = (bf16[7168,3584]{1,0:T(8,128)(2,1)}, f32[7168,1]{1,0:T(8,128)}) custom-call(bf16[7168,256]{1,0:T(8,128)(2,1)} %all-gather.4.cloned.1.call-done.a_ref, bf16[3584,256]{1,0:T(8,128)(2,1)} %all-gather.6.cloned.1.call-done.b_ref), custom_call_target="tpu_custom_call" | custom-call | flops 13153337344 | bytes 51380224 | tf_op jit(solution)/shard_map/make_kernel/pallas_call | solution.py:56
  373.3 34.9 %psum.42 = f32[7168]{0:T(1024)S(1)} all-reduce(f32[7168]{0:T(1024)S(1)} %reduce), channel_id=1, replica_groups=mesh['row'=4,'col'=8] {'col'}, use_global_device_ids=true, to_apply=%region_6.7 | all-reduce | flops 7168 | bytes 57344 | tf_op jit(solution)/shard_map/psum | solution.py:170
  412.3 22.9 %col_pass.3 = f32[1,3584]{1,0:T(1,128)} custom-call(bf16[7168,3584]{1,0:T(8,128)(2,1)} %get-tuple-element.7.k_ref, f32[7168,128]{1,0:T(8,128)} %broadcast_in_dim.6.r_ref), custom_call_target="tpu_custom_call" | custom-call | flops 51380224 | bytes 51380224 | tf_op jit(solution)/shard_map/col_pass/pallas_call | solution.py:124
  435.3 10.7 %psum.43 = f32[1,3584]{1,0:T(1,128)S(1)} all-reduce(f32[1,3584]{1,0:T(1,128)} %col_pass.3), channel_id=1, replica_groups=mesh['row'=4,'col'=8] {'row'}, use_global_device_ids=true, to_apply=%region_7.8 | all-reduce | flops 3584 | bytes 28672 | tf_op jit(solution)/shard_map/psum | solution.py:171
  446.6 27.8 %row_pass.2 = f32[7168,1]{1,0:T(8,128)} custom-call(bf16[7168,3584]{1,0:T(8,128)(2,1)} %get-tuple-element.7.k_ref, f32[1,3584]{1,0:T(1,128)} %broadcast_divide_fusion.4.c_ref), custom_call_target="tpu_custom_call" | custom-call | flops 51380224 | bytes 51380224 | tf_op jit(solution)/shard_map/row_pass/pallas_call | solution.py:95
  477.5 33.1 %psum.44 = f32[7168]{0:T(1024)S(1)} all-reduce(f32[7168]{0:T(1024)S(1)} %reduce.1), channel_id=1, replica_groups=mesh['row'=4,'col'=8] {'col'}, use_global_device_ids=true, to_apply=%region_8.9 | all-reduce | flops 7168 | bytes 57344 | tf_op jit(solution)/shard_map/psum | solution.py:170
  514.7 22.9 %col_pass.4 = f32[1,3584]{1,0:T(1,128)} custom-call(bf16[7168,3584]{1,0:T(8,128)(2,1)} %get-tuple-element.7.k_ref, f32[7168,128]{1,0:T(8,128)} %broadcast_in_dim.7.r_ref), custom_call_target="tpu_custom_call" | custom-call | flops 51380224 | bytes 51380224 | tf_op jit(solution)/shard_map/col_pass/pallas_call | solution.py:124
  537.7 10.7 %psum.45 = f32[1,3584]{1,0:T(1,128)S(1)} all-reduce(f32[1,3584]{1,0:T(1,128)} %col_pass.4), channel_id=1, replica_groups=mesh['row'=4,'col'=8] {'row'}, use_global_device_ids=true, to_apply=%region_9.10 | all-reduce | flops 3584 | bytes 28672 | tf_op jit(solution)/shard_map/psum | solution.py:171
  548.9 27.8 %row_pass.3 = f32[7168,1]{1,0:T(8,128)} custom-call(bf16[7168,3584]{1,0:T(8,128)(2,1)} %get-tuple-element.7.k_ref, f32[1,3584]{1,0:T(1,128)} %broadcast_divide_fusion.3.c_ref), custom_call_target="tpu_custom_call" | custom-call | flops 51380224 | bytes 51380224 | tf_op jit(solution)/shard_map/row_pass/pallas_call | solution.py:95
  579.8 33.3 %psum.46 = f32[7168]{0:T(1024)S(1)} all-reduce(f32[7168]{0:T(1024)S(1)} %reduce.2), channel_id=1, replica_groups=mesh['row'=4,'col'=8] {'col'}, use_global_device_ids=true, to_apply=%region_10.11 | all-reduce | flops 7168 | bytes 57344 | tf_op jit(solution)/shard_map/psum | solution.py:170
  617.3 22.9 %col_pass.5 = f32[1,3584]{1,0:T(1,128)} custom-call(bf16[7168,3584]{1,0:T(8,128)(2,1)} %get-tuple-element.7.k_ref, f32[7168,128]{1,0:T(8,128)} %broadcast_in_dim.8.r_ref), custom_call_target="tpu_custom_call" | custom-call | flops 51380224 | bytes 51380224 | tf_op jit(solution)/shard_map/col_pass/pallas_call | solution.py:124
  640.2 10.7 %psum.47 = f32[1,3584]{1,0:T(1,128)S(1)} all-reduce(f32[1,3584]{1,0:T(1,128)} %col_pass.5), channel_id=1, replica_groups=mesh['row'=4,'col'=8] {'row'}, use_global_device_ids=true, to_apply=%region_11.12 | all-reduce | flops 3584 | bytes 28672 | tf_op jit(solution)/shard_map/psum | solution.py:171
  658.2 22.3 %fusion = bf16[7168,256]{1,0:T(8,128)(2,1)} fusion(bf16[7168,3584]{1,0:T(8,128)(2,1)} %get-tuple-element.7.k_ref, f32[7168]{0:T(1024)S(1)} %broadcast_divide_fusion, bf16[3584,1024]{1,0:T(8,128)(2,1)S(1)} %multiply_convert_fusion), kind=kOutput, calls=%fused_computation.5 | convolution fusion | flops 13157007360 | bytes 56913920 | tf_op jit(solution)/shard_map/dot_general | solution.py:176
  680.6 23.3 %fusion.1 = bf16[7168,256]{1,0:T(8,128)(2,1)} fusion(bf16[7168,3584]{1,0:T(8,128)(2,1)} %get-tuple-element.7.k_ref, f32[7168]{0:T(1024)S(1)} %broadcast_divide_fusion, bf16[3584,1024]{1,0:T(8,128)(2,1)} %copy-done), kind=kOutput, calls=%fused_computation.6 | convolution fusion | flops 13157007360 | bytes 56913920 | tf_op jit(solution)/shard_map/dot_general | solution.py:176
  704.3 23.2 %fusion.2 = bf16[7168,256]{1,0:T(8,128)(2,1)} fusion(bf16[7168,3584]{1,0:T(8,128)(2,1)} %get-tuple-element.7.k_ref, f32[7168]{0:T(1024)S(1)} %broadcast_divide_fusion, bf16[3584,1024]{1,0:T(8,128)(2,1)} %copy-done), kind=kOutput, calls=%fused_computation.7 | convolution fusion | flops 13157007360 | bytes 56913920 | tf_op jit(solution)/shard_map/dot_general | solution.py:176
  727.6 23.1 %fusion.3 = bf16[7168,256]{1,0:T(8,128)(2,1)} fusion(bf16[7168,3584]{1,0:T(8,128)(2,1)} %get-tuple-element.7.k_ref, f32[7168]{0:T(1024)S(1)} %broadcast_divide_fusion, bf16[3584,1024]{1,0:T(8,128)(2,1)} %copy-done), kind=kOutput, calls=%fused_computation.8 | convolution fusion | flops 13157007360 | bytes 56913920 | tf_op jit(solution)/shard_map/dot_general | solution.py:176
  750.7 8.6 reduce-scatter.11.cloned.1.call-done
  759.2 84.3 %reduce-scatter.13.cloned.1.call-done = bf16[896,256]{1,0:T(8,128)(2,1)} async-done(((bf16[7168,256]{1,0:T(8,128)(2,1)}), bf16[896,256]{1,0:T(8,128)(2,1)}) %reduce-scatter.13.cloned.1.call-update) | async-done | bytes 458768 | tf_op jit(solution)/shard_map/reduce_scatter | solution.py:178
  843.6 84.4 %reduce-scatter.15.cloned.1.call-done = bf16[896,256]{1,0:T(8,128)(2,1)} async-done(((bf16[7168,256]{1,0:T(8,128)(2,1)}), bf16[896,256]{1,0:T(8,128)(2,1)}) %reduce-scatter.15.cloned.1.call-update) | async-done | bytes 458768 | tf_op jit(solution)/shard_map/reduce_scatter | solution.py:178
  928.0 84.3 %reduce-scatter.17.cloned.1.call-done = bf16[896,256]{1,0:T(8,128)(2,1)} async-done(((bf16[7168,256]{1,0:T(8,128)(2,1)}), bf16[896,256]{1,0:T(8,128)(2,1)}) %reduce-scatter.17.cloned.1.call-update) | async-done | bytes 458768 | tf_op jit(solution)/shard_map/reduce_scatter | solution.py:178
  (47 shorter events, 41.7 us)
Async XLA Ops:
  6.5 176.7 %reduce-scatter.7.cloned.1.call-start = ((), (), s32[]{:S(2)}) async-start(), calls=%async_computation.6 | async-start | bytes 8257536 | tf_op jit(solution)/shard_map/reduce_scatter | solution.py:145
  47.5 203.4 %reduce-scatter.9.cloned.1.call-start = ((), (), s32[]{:S(2)}) async-start(), calls=%async_computation.8 | async-start | bytes 9175040 | tf_op jit(solution)/shard_map/reduce_scatter | solution.py:145
  76.4 199.2 %all-gather.6.cloned.1.call-start = ((), (), s32[]{:S(2)}) async-start(), calls=%async_computation.9 | async-start | bytes 2293760 | tf_op jit(solution)/shard_map/all_gather | solution.py:147
  254.3 89.5 %all-gather.4.cloned.1.call-start = ((), (), s32[]{:S(2)}) async-start(), calls=%async_computation.7 | async-start | bytes 4128768 | tf_op jit(solution)/shard_map/all_gather | solution.py:147
  255.8 395.2 %all-gather.8.cloned.1.call-start = ((), (), s32[]{:S(2)}) async-start(), calls=%async_computation.10 | async-start | bytes 9175040 | tf_op jit(solution)/shard_map/all_gather | solution.py:164
  256.4 502.8 %reduce-scatter.11.cloned.1.call-start = ((), (), s32[]{:S(2)}) async-start(), calls=%async_computation.11 | async-start | bytes 4128768 | tf_op jit(solution)/shard_map/reduce_scatter | solution.py:178
  655.3 2.9 copy-start
  680.6 163.0 %reduce-scatter.13.cloned.1.call-start = ((), (), s32[]{:S(2)}) async-start(), calls=%async_computation.12 | async-start | bytes 4128768 | tf_op jit(solution)/shard_map/reduce_scatter | solution.py:178
  704.0 224.0 %reduce-scatter.15.cloned.1.call-start = ((), (), s32[]{:S(2)}) async-start(), calls=%async_computation.13 | async-start | bytes 4128768 | tf_op jit(solution)/shard_map/reduce_scatter | solution.py:178
  727.5 284.8 %reduce-scatter.17.cloned.1.call-start = ((), (), s32[]{:S(2)}) async-start(), calls=%async_computation.14 | async-start | bytes 4128768 | tf_op jit(solution)/shard_map/reduce_scatter | solution.py:178
  750.6 261.7 %copy-start.1 = (bf16[896,1024]{1,0:T(8,128)(2,1)S(1)}, bf16[896,1024]{1,0:T(8,128)(2,1)}, u32[]{:S(2)}) copy-start(bf16[896,1024]{1,0:T(8,128)(2,1)} %param.12) | copy-start | bytes 5505028
Sparse Core Ops, SparseCore 0:
  47.6 135.5 reduce-scatter.6
  185.7 65.0 reduce-scatter.8
  254.4 21.0 all-gather.5
  277.6 66.1 all-gather.3
  345.2 51.9 all-gather.7
  680.7 78.5 reduce-scatter.10
  762.9 80.6 reduce-scatter.12
  847.2 80.6 reduce-scatter.14
  931.6 80.6 reduce-scatter.16
where the time goes:
time: 1030 us; the launch traced here: 1020 us
  waiting for transfers between devices  523 us (51%)
  Pallas kernels  151 us (15%)
  matrix products  137 us (13%)
  blocking collectives  133 us (13%)
  other arithmetic  36.7 us (4%)
  local copies, waits for them, and re-layouts  27.3 us (3%)
  between operations  13.7 us (1%)
    reduce_scatter x4, waiting for transfers between devices, per_device(): lax.psum_scatter(part, 'col', scatter_dimension=0, tiled=True)  262 us
    reduce_scatter x2, waiting for transfers between devices, scores_of(): lax.psum_scatter(both, axis, scatter_dimension=0, tiled=False)  173 us
    psum x3, blocking collectives, per_device(): row_scale = 1.0 / lax.psum(row_part[:, 0], 'col')[:, None]  101 us
    dot_general x4, matrix products, per_device(): jnp.dot(kernel, scaled[:, cut:cut + window // 4], preferred_element_type=...  92 us
    all_gather x2, waiting for transfers between devices, scores_of(): return lax.all_gather(mine, axis, axis=0, tiled=True)  87.2 us
    pallas_call x3, Pallas kernels, col_pass(): pl.pallas_call(body, grid=(rows // block,), in_specs=[pl.BlockSpec((block...  68.8 us
    pallas_call x2, Pallas kernels, row_pass(): pl.pallas_call(body, grid=(rows // block,), in_specs=[pl.BlockSpec((block...  55.7 us
    psum x3, blocking collectives, per_device(): column_scaling = 1.0 / lax.psum(col_pass(kernel, row_scale), 'row')  32 us
  transfers between devices with their start and end apart: 9, of which 8 were waited for; matrix products, arithmetic and copies ran while one was open for 12% of the time, Pallas kernels for 15%

commit v1 on v0

v1 whole, which is shorter than its diff:
```python
import functools
import math

import jax
import jax.numpy as jnp
from jax import lax
from jax.experimental import pallas as pl
from jax.experimental.pallas import tpu as pltpu
from jax.sharding import PartitionSpec as P

ITERS = 3


softness = 0.02
statistic_floor = 1e-05
LANES = 128


def standardize(gate_pre, up_preactivation):
    hidden = jax.nn.silu(gate_pre) * up_preactivation
    center = jnp.mean(hidden, axis=0, keepdims=True)
    spread = jnp.mean(jnp.square(hidden - center), axis=0, keepdims=True)
    return ((hidden - center) * lax.rsqrt(spread + statistic_floor)).astype(jnp.bfloat16)


def block_of(size, most):
    block = most
    while size % block:
        block //= 2
    return block


def lane_chunk(size, most):
    chunk = most
    while size % chunk:
        chunk -= LANES
    return chunk


MESH = pl.DeviceIdType.MESH


def grid_of(members):
    inner = 1
    while (2 * inner) ** 2 <= members and members % (2 * inner) == 0:
        inner *= 2
    return members // inner, inner


def halves_of(vector):
    high = vector.astype(jnp.bfloat16).astype(jnp.float32)
    low = vector - high
    place = lax.broadcasted_iota(jnp.int32, (16, vector.shape[1]), 0)
    return jnp.where(place == 0, high, jnp.where(place == 1, low, 0.0)).astype(jnp.bfloat16)


def sinkhorn(scores_a, scores_b, n_row, n_col, exponent):
    rows, depth = scores_a.shape
    cols = scores_b.shape[0]
    outer, inner = grid_of(n_col)
    block = block_of(rows, 512)
    chunk = lane_chunk(cols, 512)

    def body(a_ref, b_ref, r_ref, c_ref, b_all, k_ref, rv, cv, r_send, c_send, r_recv, c_recv, pair,
             rs, rr, cs, cr, bs, br, local, ps, pr):
        me_row, me_col = lax.axis_index("row"), lax.axis_index("col")
        partner = lax.rem(me_col + n_col // 2, n_col)
        barrier = pltpu.get_barrier_semaphore()
        for j in range(1, n_col):
            pl.semaphore_signal(barrier, 1, device_id={"col": lax.rem(me_col + j, n_col)}, device_id_type=MESH)
        for j in range(1, n_row):
            pl.semaphore_signal(barrier, 1, device_id={"row": lax.rem(me_row + j, n_row)}, device_id_type=MESH)
        pl.semaphore_wait(barrier, n_col + n_row - 2)

        own_b = pltpu.make_async_copy(b_ref, b_all.at[0], local)
        own_b.start()
        pair_b = pltpu.make_async_remote_copy(
            b_ref, b_all.at[1], bs, br, device_id={"col": partner}, device_id_type=MESH)
        pair_b.start()

        def swap(step, send, recv, ssem, rsem, axis, me, n):
            copies = []
            for j in range(1, n):
                copy = pltpu.make_async_remote_copy(
                    send.at[step], recv.at[step, j], ssem.at[step, j], rsem.at[step, j],
                    device_id={axis: lax.rem(me + j, n)}, device_id_type=MESH)
                copy.start()
                copies.append(copy)
            total = send[step]
            for j, copy in enumerate(copies):
                copy.wait()
                total = total + recv[step, j + 1]
            return 1.0 / total

        def row_part(step, base):
            part = lax.dot_general(
                cv[...], k_ref[pl.ds(base, block), :], (((1,), (1,)), ((), ())),
                preferred_element_type=jnp.float32)
            r_send[step, :, pl.ds(base, block)] = part[0:1] + part[1:2]

        cv[...] = halves_of(jnp.ones((1, cols), jnp.float32))

        @pl.loop(0, rows // block)
        def _(i):
            base = pl.multiple_of(i * block, block)
            for start in range(0, cols, chunk):
                logits = lax.dot_general(
                    a_ref[pl.ds(base, block), :], b_ref[start : start + chunk, :], (((1,), (1,)), ((), ())),
                    preferred_element_type=jnp.float32)
                k_ref[pl.ds(base, block), start : start + chunk] = jnp.exp2(logits * exponent).astype(jnp.bfloat16)
            row_part(0, base)

        for step in range(ITERS):
            if step:
                @pl.loop(0, rows // block)
                def _(i):
                    row_part(step, pl.multiple_of(i * block, block))
            scale = swap(step, r_send, r_recv, rs, rr, "col", me_col, n_col)
            rv[...] = halves_of(scale)
            if step == ITERS - 1:
                r_ref[...] = scale
            c_send[step] = jnp.zeros((1, cols), jnp.float32)

            @pl.loop(0, rows // block)
            def _(i):
                base = pl.multiple_of(i * block, block)
                part = jnp.dot(
                    rv[:, pl.ds(base, block)], k_ref[pl.ds(base, block), :], preferred_element_type=jnp.float32)
                c_send[step] += part[0:1] + part[1:2]

            scale = swap(step, c_send, c_recv, cs, cr, "row", me_row, n_row)
            if step < ITERS - 1:
                cv[...] = halves_of(scale)
            else:
                pair[0] = scale
                pair_c = pltpu.make_async_remote_copy(
                    pair.at[0], pair.at[1], ps, pr, device_id={"col": partner}, device_id_type=MESH)
                pair_c.start()
                pair_c.wait()
                c_ref[...] = pair[...]
        own_b.wait()
        pair_b.wait()

    dma = pltpu.SemaphoreType.DMA
    return pl.pallas_call(
        body,
        in_specs=[pl.BlockSpec(memory_space=pltpu.VMEM)] * 2,
        out_specs=[
            pl.BlockSpec(memory_space=pltpu.VMEM),
            pl.BlockSpec(memory_space=pltpu.VMEM),
            pl.BlockSpec(memory_space=pl.ANY),
        ],
        out_shape=[
            jax.ShapeDtypeStruct((1, rows), jnp.float32),
            jax.ShapeDtypeStruct((2, 1, cols), jnp.float32),
            jax.ShapeDtypeStruct((2, cols, depth), jnp.bfloat16),
        ],
        scratch_shapes=[
            pltpu.VMEM((rows, cols), jnp.bfloat16),
            pltpu.VMEM((16, rows), jnp.bfloat16),
            pltpu.VMEM((16, cols), jnp.bfloat16),
            pltpu.VMEM((ITERS, 1, rows), jnp.float32),
            pltpu.VMEM((ITERS, 1, cols), jnp.float32),
            pltpu.VMEM((ITERS, n_col, 1, rows), jnp.float32),
            pltpu.VMEM((ITERS, n_row, 1, cols), jnp.float32),
            pltpu.VMEM((2, 1, cols), jnp.float32),
            dma((ITERS, n_col)), dma((ITERS, n_col)), dma((ITERS, n_row)), dma((ITERS, n_row)),
            dma, dma, dma, dma, dma,
        ],
        compiler_params=pltpu.CompilerParams(
            collective_id=1, has_side_effects=True, vmem_limit_bytes=67043328),
        cost_estimate=pl.CostEstimate(
            flops=2 * rows * cols * depth * 3, bytes_accessed=2 * (rows + cols) * depth, transcendentals=rows * cols),
        name="sinkhorn",
    )(scores_a, scores_b)


def join(scores_a, b_all, row_scale, col_scale, down_own, down_pair, down_a, n_col, exponent):
    rows, depth = scores_a.shape
    cols = b_all.shape[1]
    quarters, _, width = down_own.shape
    window = quarters * width
    outer, inner = grid_of(n_col)
    near = outer // 2
    group = near * inner
    half, own = rows // 2, rows // n_col
    subs = 2
    piece = own // subs
    steps = group * subs
    sent = steps - subs
    chunk = lane_chunk(cols, 512)
    pieces = cols // chunk

    def body(a_hbm, b_hbm, r_ref, c_ref, own_hbm, pair_hbm, down_ref, out_ref, a_ref, b_ref, d_ref, total, plan,
             out_buf, in_buf, local, ssem, rsem):
        me = lax.axis_index("col")
        mo, mi = me // inner, lax.rem(me, inner)
        side, near_o = mo // near, lax.rem(mo, near)

        def place(j):
            oo = lax.rem(near_o + j // inner, near)
            ii = lax.rem(mi + lax.rem(j, inner), inner)
            return (side * near + oo) * inner + ii

        barrier = pltpu.get_barrier_semaphore()
        for j in range(1, group):
            pl.semaphore_signal(barrier, 1, device_id={"col": place(j)}, device_id_type=MESH)
        loads = [
            pltpu.make_async_copy(a_hbm.at[pl.ds(pl.multiple_of(side * half, 8), half)], a_ref, local.at[0]),
            pltpu.make_async_copy(b_hbm, b_ref, local.at[1]),
            pltpu.make_async_copy(own_hbm, d_ref.at[0], local.at[2]),
            pltpu.make_async_copy(pair_hbm, d_ref.at[1], local.at[3]),
        ]
        for load in loads:
            load.start()
        for load in loads:
            load.wait()
        pl.semaphore_wait(barrier, group - 1)

        def copy_of(t, target):
            return pltpu.make_async_remote_copy(
                out_buf.at[t], in_buf.at[t], ssem.at[t], rsem.at[t],
                device_id={"col": target}, device_id_type=MESH)

        @pl.loop(0, steps)
        def _(t):
            j = (group - 1) - t // subs
            target = place(j)
            first = pl.multiple_of((target - side * group) * own + lax.rem(t, subs) * piece, math.gcd(piece, 128))
            total[...] = jnp.zeros_like(total)
            for s in range(2):
                @pl.loop(0, pieces)
                def _(k):
                    base = pl.multiple_of(k * chunk, chunk)
                    logits = lax.dot_general(
                        a_ref[pl.ds(first, piece), :], b_ref[s, pl.ds(base, chunk), :], (((1,), (1,)), ((), ())),
                        preferred_element_type=jnp.float32)
                    plan[...] = (jnp.exp2(logits * exponent) * c_ref[s, :, pl.ds(base, chunk)]).astype(jnp.bfloat16)
                    for q in range(quarters):
                        total[:, q * width : (q + 1) * width] += jnp.dot(
                            plan[...], d_ref[s, q, pl.ds(base, chunk), :], preferred_element_type=jnp.float32)
            spot = pl.multiple_of(target * own + lax.rem(t, subs) * piece, math.gcd(piece, 8))
            out_buf[t] = (total[...] * r_ref[pl.ds(spot, piece), :]).astype(jnp.bfloat16)

            @pl.when(t < sent)
            def _():
                copy_of(t, target).start()

        @pl.loop(0, subs)
        def _(u):
            summed = out_buf[sent + u].astype(jnp.float32)
            for g in range(group - 1):
                copy_of(g * subs + u, place(1)).wait_recv()
                summed = summed + in_buf[g * subs + u].astype(jnp.float32)
            spot = pl.ds(pl.multiple_of(u * piece, math.gcd(piece, 16)), piece)
            out_ref[spot, :] = ((down_ref[spot, :].astype(jnp.float32) + summed) * 0.5).astype(jnp.bfloat16)

        @pl.loop(0, sent)
        def _(t):
            copy_of(t, place((group - 1) - t // subs)).wait_send()

    dma = pltpu.SemaphoreType.DMA
    vmem, hbm = pl.BlockSpec(memory_space=pltpu.VMEM), pl.BlockSpec(memory_space=pl.ANY)
    return pl.pallas_call(
        body,
        in_specs=[hbm, hbm, vmem, vmem, hbm, hbm, vmem],
        out_specs=vmem,
        out_shape=jax.ShapeDtypeStruct((own, window), jnp.bfloat16),
        scratch_shapes=[
            pltpu.VMEM((half, depth), jnp.bfloat16),
            pltpu.VMEM((2, cols, depth), jnp.bfloat16),
            pltpu.VMEM((2, quarters, cols, width), jnp.bfloat16),
            pltpu.VMEM((piece, window), jnp.float32),
            pltpu.VMEM((piece, chunk), jnp.bfloat16),
            pltpu.VMEM((steps, piece, window), jnp.bfloat16),
            pltpu.VMEM((sent, piece, window), jnp.bfloat16),
            dma((4,)), dma((steps,)), dma((steps,)),
        ],
        compiler_params=pltpu.CompilerParams(
            collective_id=2, has_side_effects=True, vmem_limit_bytes=67043328),
        cost_estimate=pl.CostEstimate(
            flops=2 * rows * cols * (window + depth), bytes_accessed=8 * cols * window, transcendentals=rows * cols),
        name="join",
    )(scores_a, b_all, row_scale, col_scale, down_own, down_pair, down_a)


def reduced(gate_pre, up_pre, axis, parts):
    tokens, width = gate_pre.shape
    own = width // parts
    both = jnp.stack((gate_pre.astype(jnp.bfloat16), up_pre.astype(jnp.bfloat16)))
    both = both.reshape(2, tokens, parts, own).transpose(2, 0, 1, 3)
    return lax.psum_scatter(both, axis, scatter_dimension=0, tiled=False)


def scores_of(summed, axis):
    summed = summed.astype(jnp.float32)
    mine = standardize(summed[0], summed[1]).T
    return lax.all_gather(mine, axis, axis=0, tiled=True)


def solution(mesh):
    n_row, n_col = mesh.shape["row"], mesh.shape["col"]

    def per_device(calib, gate_a, up_a, gate_b, up_b, down_a, down_b):
        width_a = gate_a.shape[0]
        width_b = gate_b.shape[0]
        inputs_a = lax.dynamic_slice_in_dim(calib, lax.axis_index("col") * width_a, width_a, 1)
        inputs_b = lax.dynamic_slice_in_dim(calib, lax.axis_index("row") * width_b, width_b, 1)
        gate_pre_a = jnp.dot(inputs_a, gate_a, preferred_element_type=jnp.float32)
        up_pre_a = jnp.dot(inputs_a, up_a, preferred_element_type=jnp.float32)
        gate_pre_b = jnp.dot(inputs_b, gate_b, preferred_element_type=jnp.float32)
        up_pre_b = jnp.dot(inputs_b, up_b, preferred_element_type=jnp.float32)
        turned = [(i, (i + n_col // 2) % n_col) for i in range(n_col)]
        pair_b = lax.ppermute(down_b, "col", turned)
        summed_a = reduced(gate_pre_a, up_pre_a, "col", n_col)
        summed_a, pair_b = lax.optimization_barrier((summed_a, pair_b))
        scores_a = scores_of(summed_a, "col")
        scores_b = scores_of(reduced(gate_pre_b, up_pre_b, "row", n_row), "row")
        down_own = lax.all_gather(down_b, "row")
        down_pair = lax.all_gather(pair_b, "row")
        exponent = math.log2(math.e) / (calib.shape[0] * softness)
        row_scale, col_scale, b_all = sinkhorn(scores_a, scores_b, n_row, n_col, exponent)
        return join(
            scores_a, b_all, row_scale.reshape(-1, 1), col_scale, down_own, down_pair, down_a, n_col, exponent)

    placed = (
        P(),
        P("col", "row"),
        P("col", "row"),
        P("row", "col"),
        P("row", "col"),
        P(("row", "col"), None),
        P("col", "row"),
    )
    return jax.shard_map(
        per_device, mesh=mesh, in_specs=placed, out_specs=P(("row", "col"), None), check_vma=False
    )
```

time: 1030 us -> 667 us (0.65)
  waiting for transfers between devices: 523 us -> 281 us
  blocking collectives: 133 us -> 0 us
  Pallas kernels: 151 us -> 282 us
  matrix products: 137 us -> 44.6 us
  other arithmetic: 36.7 us -> 16.6 us
    reduce_scatter x6 -> x2, waiting for transfers between devices: 435 us -> 55.7 us  [reduced(): return lax.psum_scatter(both, axis, scatter_dimension=0, tiled=False)]
    ppermute x0 -> x1, waiting for transfers between devices: none -> 138 us  [per_device(): pair_b = lax.ppermute(down_b, 'col', turned)]
    psum x6 -> x0, blocking collectives: 133 us -> none  [the longest x3 101 us: per_device(): row_scale = 1.0 / lax.psum(row_part[:, 0], 'col')[:, None]]
    pallas_call x6 -> x2, Pallas kernels: 151 us -> 282 us  [the longest x1 172 us: sinkhorn(): pl.pallas_call(body, in_specs=[pl.BlockSpec(memory_space=pltpu.VMEM)] * 2...]
    dot_general x4 -> x0, matrix products: 92 us -> none  [per_device(): jnp.dot(kernel, scaled[:, cut:cut + window // 4], preferred_element_type=...]
    broadcast_in_dim x3 -> x0, local copies, waits for them, and re-layouts: 12.5 us -> none  [col_pass(): jnp.broadcast_to(row_scale, (rows, LANES))]
  transfers between devices with their start and end apart: 9 -> 7, of which waited for: 8 -> 4; matrix products, arithmetic and copies ran while one was open for 12% -> 7% of each run, Pallas kernels for 15% -> 26%
where the time goes in v1:
time: 667 us; the launch traced here: 666 us
  Pallas kernels  282 us (42%)
  waiting for transfers between devices  281 us (42%)
  matrix products  44.6 us (7%)
  local copies, waits for them, and re-layouts  24.6 us (4%)
  other arithmetic  16.6 us (2%)
  between operations  13.5 us (2%)
    pallas_call x1, Pallas kernels, sinkhorn(): pl.pallas_call(body, in_specs=[pl.BlockSpec(memory_space=pltpu.VMEM)] * 2...  172 us
    ppermute x1, waiting for transfers between devices, per_device(): pair_b = lax.ppermute(down_b, 'col', turned)  138 us
    pallas_call x1, Pallas kernels, join(): pl.pallas_call(body, in_specs=[hbm, hbm, vmem, vmem, hbm, hbm, vmem], out...  110 us
    all_gather x2, waiting for transfers between devices, scores_of(): return lax.all_gather(mine, axis, axis=0, tiled=True)  86 us
    reduce_scatter x2, waiting for transfers between devices, reduced(): return lax.psum_scatter(both, axis, scatter_dimension=0, tiled=False)  55.7 us
  transfers between devices with their start and end apart: 7, of which 4 were waited for; matrix products, arithmetic and copies ran while one was open for 7% of the time, Pallas kernels for 26%

profile of v1, /device:TPU:0, one launch (start us, length us, event | category | flops | bytes accessed | tf_op | source)
XLA Modules:
  0.0 666.3 jit_solution(4733406960979750747)
XLA Ops:
  6.5 10.7 %convolution_convert_fusion.3 = bf16[256,3584]{1,0:T(8,128)(2,1)} fusion(bf16[2048,3584]{1,0:T(8,128)(2,1)} %param.10, bf16[256,8192]{1,0:T(8,128)(2,1)} %param.7, s32[]{:T(128)S(6)} %select_n.7), kind=kOutput, calls=%fused_computation.4 | convolution fusion | flops 3759013888 | bytes 17563652 | tf_op jit(solution)/shard_map/dot_general | solution.py:311
  17.2 2.9 copy.14
  20.1 10.7 %convolution_convert_fusion.2 = bf16[256,3584]{1,0:T(8,128)(2,1)} fusion(bf16[2048,3584]{1,0:T(8,128)(2,1)} %param.11, bf16[256,8192]{1,0:T(8,128)(2,1)} %param.7, s32[]{:T(128)S(6)} %select_n.7), kind=kOutput, calls=%fused_computation.3 | convolution fusion | flops 3759013888 | bytes 17563652 | tf_op jit(solution)/shard_map/dot_general | solution.py:312
  30.8 3.8 copy.15
  34.6 3.7 maximum_bitcast_fusion.1
  38.4 0.2 reduce-scatter.3.cloned.1.call-start
  38.6 11.5 %convolution_convert_fusion.1 = bf16[256,7168]{1,0:T(8,128)(2,1)} fusion(bf16[1024,7168]{1,0:T(8,128)(2,1)} %param.8, bf16[256,8192]{1,0:T(8,128)(2,1)} %param.7, s32[]{:T(128)S(6)} %select_n.6), kind=kOutput, calls=%fused_computation.1 | convolution fusion | flops 3759931392 | bytes 18874372 | tf_op jit(solution)/shard_map/dot_general | solution.py:309
  50.1 6.0 copy.12
  56.0 11.7 %convolution_convert_fusion = bf16[256,7168]{1,0:T(8,128)(2,1)} fusion(bf16[1024,7168]{1,0:T(8,128)(2,1)} %param.9, bf16[256,8192]{1,0:T(8,128)(2,1)} %param.7, s32[]{:T(128)S(6)} %select_n.6), kind=kOutput, calls=%fused_computation | convolution fusion | flops 3759931392 | bytes 18874372 | tf_op jit(solution)/shard_map/dot_general | solution.py:310
  67.8 5.9 copy.13
  73.7 6.8 %maximum_bitcast_fusion = bf16[8,2,256,896]{2,3,1,0:T(8,128)(2,1)} fusion(bf16[1,256,8,896]{1,3,0,2:T(8,128)(2,1)} %bitcast.41, bf16[1,256,8,896]{1,3,0,2:T(8,128)(2,1)} %bitcast.40), kind=kLoop, calls=%fused_computation.2 | loop fusion | flops 3670016 | bytes 14680064 | tf_op jit(solution)/shard_map/transpose | solution.py:291
  80.5 0.0 all-gather.9.cloned.1.call-start
  80.6 3.8 collective-permute-start
  84.4 1.3 convert_element_type.31
  85.7 138.0 %collective-permute-done = bf16[3584,256]{1,0:T(8,128)(2,1)} collective-permute-done((bf16[3584,256]{1,0:T(8,128)(2,1)}, bf16[3584,256]{1,0:T(8,128)(2,1)}, u32[]{:S(2)}, u32[]{:S(2)}) %collective-permute-start) | collective-permute-done | bytes 1835040 | tf_op jit(solution)/shard_map/ppermute | solution.py:314
  223.7 55.7 %reduce-scatter.3.cloned.1.call-done = bf16[1,2,256,896]{2,3,1,0:T(8,128)(2,1)} async-done(((bf16[8,2,256,896]{2,3,1,0:T(8,128)(2,1)}), bf16[1,2,256,896]{2,3,1,0:T(8,128)(2,1)}) %reduce-scatter.3.cloned.1.call-update) | async-done | bytes 917520 | tf_op jit(solution)/shard_map/reduce_scatter | solution.py:292
  279.4 1.3 convert_element_type.27
  280.7 0.6 fusion.12
  281.3 0.3 multiply_reduce_fusion
  281.6 1.1 fusion.7
  282.7 0.0 all-gather.7.cloned.1.call-start
  282.8 0.3 multiply_reduce_fusion.1
  283.2 1.1 fusion.6
  284.3 0.5 all-gather.11.cloned.1.call-update
  284.9 0.3 all-gather.13.cloned.1.call-start
  285.1 0.3 all-gather.13.cloned.1.call-update
  285.4 17.7 %all-gather.9.cloned.1.call-done.b_ref = bf16[3584,256]{1,0:T(8,128)(2,1)} async-done(((bf16[896,256]{1,0:T(8,128)(2,1)}), bf16[3584,256]{1,0:T(8,128)(2,1)}) %all-gather.9.cloned.1.call-update) | async-done | bytes 1835024 | tf_op jit(solution)/shard_map/all_gather | solution.py:298
  303.1 68.3 %all-gather.7.cloned.1.call-done.a_ref.a_hbm = bf16[7168,256]{1,0:T(8,128)(2,1)} async-done(((bf16[896,256]{1,0:T(8,128)(2,1)}), bf16[7168,256]{1,0:T(8,128)(2,1)}) %all-gather.7.cloned.1.call-update) | async-done | bytes 3670032 | tf_op jit(solution)/shard_map/all_gather | solution.py:298
  371.4 172.3 %sinkhorn.1 = (f32[1,7168]{1,0:T(1,128)}, f32[2,1,3584]{2,1,0:T(1,128)}, bf16[2,3584,256]{2,1,0:T(8,128)(2,1)}) custom-call(bf16[7168,256]{1,0:T(8,128)(2,1)} %all-gather.7.cloned.1.call-done.a_ref.a_hbm, bf16[3584,256]{1,0:T(8,128)(2,1)} %all-gather.9.cloned.1.call-done.b_ref), custom_call_target="tpu_custom_call" | custom-call | flops 39460012032 | bytes 5505024 | tf_op jit(solution)/shard_map/sinkhorn/pallas_call | solution.py:145
  543.7 3.2 copy.16.r_ref
  546.9 109.7 %join.1 = bf16[896,1024]{1,0:T(8,128)(2,1)} custom-call(bf16[7168,256]{1,0:T(8,128)(2,1)} %all-gather.7.cloned.1.call-done.a_ref.a_hbm, bf16[2,3584,256]{2,1,0:T(8,128)(2,1)} %get-tuple-element.11.b_hbm, f32[7168,1]{1,0:T(8,128)} %copy.16.r_ref, f32[2,1,3584]{2,1,0:T(1,128)} %get-tuple-element.13.c_ref, bf16[4,3584,256]{2,1,0:T(8,128)(2,1)} %bitcast.46, ...), custom_call_target="tpu_custom_call" | custom-call | flops 65766686720 | bytes 29360128 | tf_op jit(solution)/shard_map/join/pallas_call | solution.py:264
  656.5 2.9 copy.18
  (13 shorter events, 0.1 us)
Async XLA Ops:
  6.5 77.8 %reduce-scatter.5.cloned.1.call-start = ((), (), s32[]{:S(2)}) async-start(), calls=%async_computation.4 | async-start | bytes 4587520 | tf_op jit(solution)/shard_map/reduce_scatter | solution.py:292
  38.4 241.0 %reduce-scatter.3.cloned.1.call-start = ((), (), s32[]{:S(2)}) async-start(), calls=%async_computation.2 | async-start | bytes 8257536 | tf_op jit(solution)/shard_map/reduce_scatter | solution.py:292
  80.5 222.6 %all-gather.9.cloned.1.call-start = ((), (), s32[]{:S(2)}) async-start(), calls=%async_computation.5 | async-start | bytes 2293760 | tf_op jit(solution)/shard_map/all_gather | solution.py:298
  80.6 143.2 %collective-permute-start = (bf16[3584,256]{1,0:T(8,128)(2,1)}, bf16[3584,256]{1,0:T(8,128)(2,1)}, u32[]{:S(2)}, u32[]{:S(2)}) collective-permute-start(bf16[3584,256]{1,0:T(8,128)(2,1)} %param.13), channel_id=1, source_target_pairs={{0,4},{1,5},{2,6},{3,7},{4,0},{5,1},{6,2},{7,3},{8,12},{9,13},{10,... | collective-permute-start | bytes 5505032 | tf_op jit(solution)/shard_map/ppermute | solution.py:314
  282.7 88.6 %all-gather.7.cloned.1.call-start = ((), (), s32[]{:S(2)}) async-start(), calls=%async_computation.3 | async-start | bytes 4128768 | tf_op jit(solution)/shard_map/all_gather | solution.py:298
  284.3 262.6 %all-gather.11.cloned.1.call-start = ((), (), s32[]{:S(2)}) async-start(), calls=%async_computation.6 | async-start | bytes 9175040 | tf_op jit(solution)/shard_map/all_gather | solution.py:319
  284.9 262.0 %all-gather.13.cloned.1.call-start = ((), (), s32[]{:S(2)}) async-start(), calls=%async_computation.7 | async-start | bytes 9175040 | tf_op jit(solution)/shard_map/all_gather | solution.py:320
Sparse Core Ops, SparseCore 0:
  38.5 43.9 reduce-scatter.4
  86.1 193.2 reduce-scatter.2
  282.9 20.1 all-gather.8
  305.1 66.1 all-gather.6
  372.8 51.0 all-gather.10
  425.3 52.9 all-gather.12

commit v2 on v1

--- a/solution.py
+++ b/solution.py
@@ -54,68 +54,179 @@
     return jnp.where(place == 0, high, jnp.where(place == 1, low, 0.0)).astype(jnp.bfloat16)
 
 
-def sinkhorn(scores_a, scores_b, n_row, n_col, exponent):
-    rows, depth = scores_a.shape
-    cols = scores_b.shape[0]
+def sinkhorn(mine_a, mine_b, down_b, n_row, n_col, exponent):
+    own, depth = mine_a.shape
+    own_b = mine_b.shape[0]
+    cols, width = down_b.shape
+    rows = own * n_col
     outer, inner = grid_of(n_col)
+    row_outer, row_inner = grid_of(n_row)
     block = block_of(rows, 512)
     chunk = lane_chunk(cols, 512)
-
-    def body(a_ref, b_ref, r_ref, c_ref, b_all, k_ref, rv, cv, r_send, c_send, r_recv, c_recv, pair,
-             rs, rr, cs, cr, bs, br, local, ps, pr):
+    fused = own % LANES == 0
+    cut = cols // 2
+
+    def body(a_ref, b_ref, down_ref, r_ref, c_ref, a_out, b_all, d_pair, k_ref, a_all, b_own, rv, cv,
+             r_send, c_send, r_recv, c_recv, pair, rs, rr, cs, cr, gs, gr, zs, zr, xs, xr,
+             hs, hr, ys, yr, ks, kr, local):
         me_row, me_col = lax.axis_index("row"), lax.axis_index("col")
         partner = lax.rem(me_col + n_col // 2, n_col)
+        mo, mi = me_col // inner, lax.rem(me_col, inner)
+        ro, ri = me_row // row_inner, lax.rem(me_row, row_inner)
         barrier = pltpu.get_barrier_semaphore()
         for j in range(1, n_col):
             pl.semaphore_signal(barrier, 1, device_id={"col": lax.rem(me_col + j, n_col)}, device_id_type=MESH)
         for j in range(1, n_row):
             pl.semaphore_signal(barrier, 1, device_id={"row": lax.rem(me_row + j, n_row)}, device_id_type=MESH)
+        keep_a = pltpu.make_async_copy(a_ref, a_all.at[me_col], local.at[0])
+        keep_b = pltpu.make_async_copy(b_ref, b_own.at[me_row], local.at[1])
+        keep_a.start()
+        keep_b.start()
         pl.semaphore_wait(barrier, n_col + n_row - 2)
 
-        own_b = pltpu.make_async_copy(b_ref, b_all.at[0], local)
-        own_b.start()
-        pair_b = pltpu.make_async_remote_copy(
-            b_ref, b_all.at[1], bs, br, device_id={"col": partner}, device_id_type=MESH)
-        pair_b.start()
+        def remote(src, dst, ssem, rsem, axis, target):
+            copy = pltpu.make_async_remote_copy(
+                src, dst, ssem, rsem, device_id={axis: target}, device_id_type=MESH)
+            copy.start()
+            return copy
+
+        sends = []
+        along, across = [], {}
+        for j in range(1, outer):
+            along.append(remote(a_ref, a_all.at[me_col], zs.at[j], zr.at[j], "col",
+                                lax.rem(mo + j, outer) * inner + mi))
+        for i in range(1, inner):
+            across[0, i] = remote(a_ref, a_all.at[me_col], xs.at[0, i], xr.at[0, i], "col",
+                                  mo * inner + lax.rem(mi + i, inner))
+        gather_b = [
+            remote(b_ref, b_own.at[me_row], gs.at[j], gr.at[j], "row", lax.rem(me_row + j, n_row))
+            for j in range(1, n_row)
+        ]
+
+        def source(j, i):
+            return lax.rem(mo + outer - j, outer) * inner + lax.rem(mi + inner - i, inner)
+
+        def pass_on(j):
+            along[j - 1].wait_recv()
+            spot = source(j, 0)
+            for i in range(1, inner):
+                across[j, i] = remote(a_all.at[spot], a_all.at[spot], xs.at[j, i], xr.at[j, i], "col",
+                                      mo * inner + lax.rem(mi + i, inner))
+
+        cv[...] = halves_of(jnp.ones((1, cols), jnp.float32))
+
+        def row_part(step, base, size):
+            part = lax.dot_general(
+                cv[...], k_ref[pl.ds(base, size), :], (((1,), (1,)), ((), ())),
+                preferred_element_type=jnp.float32)
+            r_send[step, :, pl.ds(base, size)] = part[0:1] + part[1:2]
+
+        def build(spot):
+            base = pl.multiple_of(spot * own, math.gcd(own, 128))
+            if own_b % LANES == 0:
+                span = LANES if own_b % 256 else 256
+                per = own_b // span
+
+                @pl.loop(0, n_row * per)
+                def _(n):
+                    m, inside = n // per, lax.rem(n, per)
+                    logits = lax.dot_general(
+                        a_all[spot], b_own[m, pl.ds(pl.multiple_of(inside * span, span), span), :],
+                        (((1,), (1,)), ((), ())), preferred_element_type=jnp.float32)
+                    k_ref[pl.ds(base, own), pl.ds(pl.multiple_of(n * span, span), span)] = jnp.exp2(
+                        logits * exponent).astype(jnp.bfloat16)
+            else:
+                for m in range(n_row):
+                    logits = lax.dot_general(
+                        a_all[spot], b_own[m], (((1,), (1,)), ((), ())), preferred_element_type=jnp.float32)
+                    k_ref[pl.ds(base, own), m * own_b : (m + 1) * own_b] = jnp.exp2(
+                        logits * exponent).astype(jnp.bfloat16)
+            if fused:
+                row_part(0, base, own)
+
+        def items():
+            return [
+                (b_ref, lambda row: b_all.at[1, row]),
+                (down_ref.at[0:cut], lambda row: d_pair.at[row, 0:cut]),
+                (down_ref.at[cut:cols], lambda row: d_pair.at[row, cut:cols]),
+            ]
+
+        hops, turns, cores = [], {}, {}
+
+        def to_partner():
+            for n, (src, dst) in enumerate(items()):
+                hops.append(remote(src, dst(me_row), hs.at[n], hr.at[n], "col", partner))
+
+        def core_sends(n, j, row):
+            ref = items()[n][1](row)
+            for i in range(1, row_inner):
+                cores[n, j, i] = remote(ref, ref, ks.at[n, j, i], kr.at[n, j, i], "row",
+                                        ro * row_inner + lax.rem(ri + i, row_inner))
+
+        def relay(n):
+            hops[n].wait_recv()
+            ref = items()[n][1](me_row)
+            for j in range(1, row_outer):
+                turns[n, j] = remote(ref, ref, ys.at[n, j], yr.at[n, j], "row",
+                                     lax.rem(ro + j, row_outer) * row_inner + ri)
+            core_sends(n, 0, me_row)
+
+        def spread(n):
+            for j in range(1, row_outer):
+                turns[n, j].wait_recv()
+                core_sends(n, j, lax.rem(ro + row_outer - j, row_outer) * row_inner + ri)
+
+        pass_on(1)
+        keep_a.wait()
+        keep_b.wait()
+        for copy in gather_b:
+            copy.wait_recv()
+        for m in range(n_row):
+            pltpu.make_async_copy(b_own.at[m], b_all.at[0, m], local.at[2 + m]).start()
+        build(me_col)
+        for i in range(1, inner):
+            across[0, i].wait_recv()
+            build(source(0, i))
+        for j in range(2, outer):
+            pass_on(j)
+            if j == outer - 1:
+                to_partner()
+            build(source(j - 1, 0))
+        build(source(outer - 1, 0))
+        for j in range(1, outer):
+            for i in range(1, inner):
+                across[j, i].wait_recv()
+                build(source(j, i))
+        side = mo // (outer // 2)
+        half_a = pltpu.make_async_copy(
+            a_all.at[pl.ds(side * (n_col // 2), n_col // 2)], a_out, local.at[2 + n_row])
+        half_a.start()
 
         def swap(step, send, recv, ssem, rsem, axis, me, n):
-            copies = []
-            for j in range(1, n):
-                copy = pltpu.make_async_remote_copy(
-                    send.at[step], recv.at[step, j], ssem.at[step, j], rsem.at[step, j],
-                    device_id={axis: lax.rem(me + j, n)}, device_id_type=MESH)
-                copy.start()
-                copies.append(copy)
+            copies = [
+                remote(send.at[step], recv.at[step, j], ssem.at[step, j], rsem.at[step, j], axis, lax.rem(me + j, n))
+                for j in range(1, n)
+            ]
             total = send[step]
             for j, copy in enumerate(copies):
                 copy.wait()
                 total = total + recv[step, j + 1]
             return 1.0 / total
 
-        def row_part(step, base):
-            part = lax.dot_general(
-                cv[...], k_ref[pl.ds(base, block), :], (((1,), (1,)), ((), ())),
-                preferred_element_type=jnp.float32)
-            r_send[step, :, pl.ds(base, block)] = part[0:1] + part[1:2]
-
-        cv[...] = halves_of(jnp.ones((1, cols), jnp.float32))
-
-        @pl.loop(0, rows // block)
-        def _(i):
-            base = pl.multiple_of(i * block, block)
-            for start in range(0, cols, chunk):
-                logits = lax.dot_general(
-                    a_ref[pl.ds(base, block), :], b_ref[start : start + chunk, :], (((1,), (1,)), ((), ())),
-                    preferred_element_type=jnp.float32)
-                k_ref[pl.ds(base, block), start : start + chunk] = jnp.exp2(logits * exponent).astype(jnp.bfloat16)
-            row_part(0, base)
-
         for step in range(ITERS):
-            if step:
+            if step or not fused:
                 @pl.loop(0, rows // block)
                 def _(i):
-                    row_part(step, pl.multiple_of(i * block, block))
+                    row_part(step, pl.multiple_of(i * block, block), block)
             scale = swap(step, r_send, r_recv, rs, rr, "col", me_col, n_col)
+            if step == 0:
+                relay(0)
+            if step == 1:
+                relay(1)
+                spread(0)
+            if step == 2:
+                spread(1)
+                relay(2)
             rv[...] = halves_of(scale)
             if step == ITERS - 1:
                 r_ref[...] = scale
@@ -131,32 +242,36 @@
             scale = swap(step, c_send, c_recv, cs, cr, "row", me_row, n_row)
             if step < ITERS - 1:
                 cv[...] = halves_of(scale)
-            else:
-                pair[0] = scale
-                pair_c = pltpu.make_async_remote_copy(
-                    pair.at[0], pair.at[1], ps, pr, device_id={"col": partner}, device_id_type=MESH)
-                pair_c.start()
-                pair_c.wait()
-                c_ref[...] = pair[...]
-        own_b.wait()
-        pair_b.wait()
+        spread(2)
+        pair[0] = scale
+        pair_c = remote(pair.at[0], pair.at[1], hs.at[3], hr.at[3], "col", partner)
+        pair_c.wait()
+        c_ref[...] = pair[...]
+        for copy in along + list(across.values()) + gather_b + hops + list(turns.values()):
+            copy.wait_send()
+        for copy in cores.values():
+            copy.wait()
+        half_a.wait()
+        for m in range(n_row):
+            pltpu.make_async_copy(b_own.at[m], b_all.at[0, m], local.at[2 + m]).wait()
 
     dma = pltpu.SemaphoreType.DMA
+    vmem, hbm = pl.BlockSpec(memory_space=pltpu.VMEM), pl.BlockSpec(memory_space=pl.ANY)
     return pl.pallas_call(
         body,
-        in_specs=[pl.BlockSpec(memory_space=pltpu.VMEM)] * 2,
-        out_specs=[
-            pl.BlockSpec(memory_space=pltpu.VMEM),
-            pl.BlockSpec(memory_space=pltpu.VMEM),
-            pl.BlockSpec(memory_space=pl.ANY),
-        ],
+        in_specs=[vmem, vmem, hbm],
+        out_specs=[vmem, vmem, hbm, hbm, hbm],
         out_shape=[
             jax.ShapeDtypeStruct((1, rows), jnp.float32),
             jax.ShapeDtypeStruct((2, 1, cols), jnp.float32),
-            jax.ShapeDtypeStruct((2, cols, depth), jnp.bfloat16),
+            jax.ShapeDtypeStruct((n_col // 2, own, depth), jnp.bfloat16),
+            jax.ShapeDtypeStruct((2, n_row, own_b, depth), jnp.bfloat16),
+            jax.ShapeDtypeStruct((n_row, cols, width), jnp.bfloat16),
         ],
         scratch_shapes=[
             pltpu.VMEM((rows, cols), jnp.bfloat16),
+            pltpu.VMEM((n_col, own, depth), jnp.bfloat16),
+            pltpu.VMEM((n_row, own_b, depth), jnp.bfloat16),
             pltpu.VMEM((16, rows), jnp.bfloat16),
             pltpu.VMEM((16, cols), jnp.bfloat16),
             pltpu.VMEM((ITERS, 1, rows), jnp.float32),
@@ -165,25 +280,29 @@
             pltpu.VMEM((ITERS, n_row, 1, cols), jnp.float32),
             pltpu.VMEM((2, 1, cols), jnp.float32),
             dma((ITERS, n_col)), dma((ITERS, n_col)), dma((ITERS, n_row)), dma((ITERS, n_row)),
-            dma, dma, dma, dma, dma,
+            dma((n_row,)), dma((n_row,)), dma((outer,)), dma((outer,)),
+            dma((outer, inner)), dma((outer, inner)),
+            dma((4,)), dma((4,)), dma((3, row_outer)), dma((3, row_outer)),
+            dma((3, row_outer, row_inner)), dma((3, row_outer, row_inner)), dma((3 + n_row,)),
         ],
         compiler_params=pltpu.CompilerParams(
             collective_id=1, has_side_effects=True, vmem_limit_bytes=67043328),
         cost_estimate=pl.CostEstimate(
             flops=2 * rows * cols * depth * 3, bytes_accessed=2 * (rows + cols) * depth, transcendentals=rows * cols),
         name="sinkhorn",
-    )(scores_a, scores_b)
+    )(mine_a, mine_b, down_b)
 
 
 def join(scores_a, b_all, row_scale, col_scale, down_own, down_pair, down_a, n_col, exponent):
-    rows, depth = scores_a.shape
+    half, depth = scores_a.shape
+    rows = 2 * half
     cols = b_all.shape[1]
     quarters, _, width = down_own.shape
     window = quarters * width
     outer, inner = grid_of(n_col)
     near = outer // 2
     group = near * inner
-    half, own = rows // 2, rows // n_col
+    own = rows // n_col
     subs = 2
     piece = own // subs
     steps = group * subs
@@ -206,7 +325,7 @@
         for j in range(1, group):
             pl.semaphore_signal(barrier, 1, device_id={"col": place(j)}, device_id_type=MESH)
         loads = [
-            pltpu.make_async_copy(a_hbm.at[pl.ds(pl.multiple_of(side * half, 8), half)], a_ref, local.at[0]),
+            pltpu.make_async_copy(a_hbm, a_ref, local.at[0]),
             pltpu.make_async_copy(b_hbm, b_ref, local.at[1]),
             pltpu.make_async_copy(own_hbm, d_ref.at[0], local.at[2]),
             pltpu.make_async_copy(pair_hbm, d_ref.at[1], local.at[3]),
@@ -292,10 +411,9 @@
     return lax.psum_scatter(both, axis, scatter_dimension=0, tiled=False)
 
 
-def scores_of(summed, axis):
+def scores_of(summed):
     summed = summed.astype(jnp.float32)
-    mine = standardize(summed[0], summed[1]).T
-    return lax.all_gather(mine, axis, axis=0, tiled=True)
+    return standardize(summed[0], summed[1]).T
 
 
 def solution(mesh):
@@ -310,18 +428,15 @@
         up_pre_a = jnp.dot(inputs_a, up_a, preferred_element_type=jnp.float32)
         gate_pre_b = jnp.dot(inputs_b, gate_b, preferred_element_type=jnp.float32)
         up_pre_b = jnp.dot(inputs_b, up_b, preferred_element_type=jnp.float32)
-        turned = [(i, (i + n_col // 2) % n_col) for i in range(n_col)]
-        pair_b = lax.ppermute(down_b, "col", turned)
-        summed_a = reduced(gate_pre_a, up_pre_a, "col", n_col)
-        summed_a, pair_b = lax.optimization_barrier((summed_a, pair_b))
-        scores_a = scores_of(summed_a, "col")
-        scores_b = scores_of(reduced(gate_pre_b, up_pre_b, "row", n_row), "row")
+        mine_b = scores_of(reduced(gate_pre_b, up_pre_b, "row", n_row))
+        mine_a = scores_of(reduced(gate_pre_a, up_pre_a, "col", n_col))
         down_own = lax.all_gather(down_b, "row")
-        down_pair = lax.all_gather(pair_b, "row")
         exponent = math.log2(math.e) / (calib.shape[0] * softness)
-        row_scale, col_scale, b_all = sinkhorn(scores_a, scores_b, n_row, n_col, exponent)
+        row_scale, col_scale, a_half, b_all, down_pair = sinkhorn(mine_a, mine_b, down_b, n_row, n_col, exponent)
+        depth = calib.shape[0]
         return join(
-            scores_a, b_all, row_scale.reshape(-1, 1), col_scale, down_own, down_pair, down_a, n_col, exponent)
+            a_half.reshape(-1, depth), b_all.reshape(2, -1, depth), row_scale.reshape(-1, 1), col_scale,
+            down_own, down_pair, down_a, n_col, exponent)
 
     placed = (
         P(),

time: 667 us -> 611 us (0.916)
  waiting for transfers between devices: 281 us -> 137 us
  Pallas kernels: 282 us -> 374 us
    ppermute x1 -> x0, waiting for transfers between devices: 138 us -> none  [per_device(): pair_b = lax.ppermute(down_b, 'col', turned)]
    pallas_call x1, Pallas kernels: 172 us -> 264 us  [sinkhorn(): pl.pallas_call(body, in_specs=[vmem, vmem, hbm], out_specs=[vmem, vmem, h...]
    all_gather x3 -> x0, waiting for transfers between devices: 86 us -> none  [the longest x2 86 us: scores_of(): return lax.all_gather(mine, axis, axis=0, tiled=True)]
    reduce_scatter x2, waiting for transfers between devices: 55.7 us -> 136 us  [reduced(): return lax.psum_scatter(both, axis, scatter_dimension=0, tiled=False)]
  transfers between devices with their start and end apart: 7 -> 3, of which waited for: 4 -> 2; matrix products, arithmetic and copies ran while one was open for 7% -> 8% of each run, Pallas kernels for 26% -> 43%
where the time goes in v2:
time: 611 us; the launch traced here: 610 us
  Pallas kernels  374 us (61%)
  waiting for transfers between devices  137 us (22%)
  matrix products  44.7 us (7%)
  local copies, waits for them, and re-layouts  24.7 us (4%)
  other arithmetic  16.5 us (3%)
  between operations  13.2 us (2%)
    pallas_call x1, Pallas kernels, sinkhorn(): pl.pallas_call(body, in_specs=[vmem, vmem, hbm], out_specs=[vmem, vmem, h...  264 us
    reduce_scatter x2, waiting for transfers between devices, reduced(): return lax.psum_scatter(both, axis, scatter_dimension=0, tiled=False)  136 us
    pallas_call x1, Pallas kernels, join(): pl.pallas_call(body, in_specs=[hbm, hbm, vmem, vmem, hbm, hbm, vmem], out...  110 us
  transfers between devices with their start and end apart: 3, of which 2 were waited for; matrix products, arithmetic and copies ran while one was open for 8% of the time, Pallas kernels for 43%

profile of v2, /device:TPU:0, one launch (start us, length us, event | category | flops | bytes accessed | tf_op | source)
XLA Modules:
  0.0 609.9 jit_solution(4101918223690242055)
XLA Ops:
  6.5 0.0 reduce-scatter.5.cloned.1.call-start
  6.5 10.7 %convolution_convert_fusion.3 = bf16[256,3584]{1,0:T(8,128)(2,1)} fusion(bf16[2048,3584]{1,0:T(8,128)(2,1)} %param.10, bf16[256,8192]{1,0:T(8,128)(2,1)} %param.7, s32[]{:T(128)S(6)} %select_n.7), kind=kOutput, calls=%fused_computation.4 | convolution fusion | flops 3759013888 | bytes 17563652 | tf_op jit(solution)/shard_map/dot_general | solution.py:429
  17.2 2.9 copy.14
  20.1 10.7 %convolution_convert_fusion.2 = bf16[256,3584]{1,0:T(8,128)(2,1)} fusion(bf16[2048,3584]{1,0:T(8,128)(2,1)} %param.11, bf16[256,8192]{1,0:T(8,128)(2,1)} %param.7, s32[]{:T(128)S(6)} %select_n.7), kind=kOutput, calls=%fused_computation.3 | convolution fusion | flops 3759013888 | bytes 17563652 | tf_op jit(solution)/shard_map/dot_general | solution.py:430
  30.8 3.8 copy.15
  34.6 3.6 maximum_bitcast_fusion.1
  38.3 0.0 reduce-scatter.5.cloned.1.call-update
  38.3 0.2 reduce-scatter.3.cloned.1.call-start
  38.5 11.5 %convolution_convert_fusion.1 = bf16[256,7168]{1,0:T(8,128)(2,1)} fusion(bf16[1024,7168]{1,0:T(8,128)(2,1)} %param.8, bf16[256,8192]{1,0:T(8,128)(2,1)} %param.7, s32[]{:T(128)S(6)} %select_n.6), kind=kOutput, calls=%fused_computation.1 | convolution fusion | flops 3759931392 | bytes 18874372 | tf_op jit(solution)/shard_map/dot_general | solution.py:427
  50.0 6.0 copy.12
  56.0 11.8 %convolution_convert_fusion = bf16[256,7168]{1,0:T(8,128)(2,1)} fusion(bf16[1024,7168]{1,0:T(8,128)(2,1)} %param.9, bf16[256,8192]{1,0:T(8,128)(2,1)} %param.7, s32[]{:T(128)S(6)} %select_n.6), kind=kOutput, calls=%fused_computation | convolution fusion | flops 3759931392 | bytes 18874372 | tf_op jit(solution)/shard_map/dot_general | solution.py:428
  67.8 5.9 copy.13
  73.7 6.9 %maximum_bitcast_fusion = bf16[8,2,256,896]{2,3,1,0:T(8,128)(2,1)} fusion(bf16[1,256,8,896]{1,3,0,2:T(8,128)(2,1)} %bitcast.41, bf16[1,256,8,896]{1,3,0,2:T(8,128)(2,1)} %bitcast.40), kind=kLoop, calls=%fused_computation.2 | loop fusion | flops 3670016 | bytes 14680064 | tf_op jit(solution)/shard_map/transpose | solution.py:410
  80.6 0.0 reduce-scatter.3.cloned.1.call-update
  80.6 0.0 all-gather.3.cloned.1.call-start
  80.7 0.7 all-gather.3.cloned.1.call-update
  81.4 1.1 reduce-scatter.5.cloned.1.call-done
  82.4 1.3 convert_element_type.32
  83.7 135.2 %reduce-scatter.3.cloned.1.call-done = bf16[1,2,256,896]{2,3,1,0:T(8,128)(2,1)} async-done(((bf16[8,2,256,896]{2,3,1,0:T(8,128)(2,1)}), bf16[1,2,256,896]{2,3,1,0:T(8,128)(2,1)}) %reduce-scatter.3.cloned.1.call-update) | async-done | bytes 917520 | tf_op jit(solution)/shard_map/reduce_scatter | solution.py:411
  218.9 1.3 convert_element_type.28
  220.2 0.6 fusion.12
  220.8 0.3 multiply_reduce_fusion.1
  221.2 0.3 multiply_reduce_fusion
  221.5 1.1 fusion.6.a_ref
  222.6 1.1 fusion.7.b_ref
  223.7 263.8 %sinkhorn.1 = (f32[1,7168]{1,0:T(1,128)}, f32[2,1,3584]{2,1,0:T(1,128)}, bf16[4,896,256]{2,1,0:T(8,128)(2,1)}, bf16[2,4,896,256]{3,2,1,0:T(8,128)(2,1)}, bf16[4,3584,256]{2,1,0:T(8,128)(2,1)}) custom-call(bf16[896,256]{1,0:T(8,128)(2,1)} %fusion.6.a_ref, bf16[896,256]{1,0:T(8,128)(2,1)} %fusion.7.b_ref, bf16[3584,256]{1,0:T(8,128)(2,1)} %down_ref.2), custom_call_target="tpu_custom_call" | custom-call | flops 39460012032 | bytes 5505024 | tf_op jit(solution)/shard_map/sinkhorn/pallas_call | solution.py:260
  487.5 3.2 copy.16.r_ref
  490.7 0.0 all-gather.3.cloned.1.call-done
  490.7 109.8 %join.1 = bf16[896,1024]{1,0:T(8,128)(2,1)} custom-call(bf16[3584,256]{1,0:T(8,128)(2,1)} %bitcast.47, bf16[2,3584,256]{2,1,0:T(8,128)(2,1)} %bitcast.46, f32[7168,1]{1,0:T(8,128)} %copy.16.r_ref, f32[2,1,3584]{2,1,0:T(1,128)} %get-tuple-element.13.c_ref, bf16[4,3584,256]{2,1,0:T(8,128)(2,1)} %bitcast.45, bf16[4,3584,256]{2,1,0:T(8,128)(2,1)} %get-tuple-element.14.pair_hbm, ...), custom_call_target="tpu_custom_call" | custom-call | flops 65766686720 | bytes 29360128 | tf_op jit(solution)/shard_map/join/pallas_call | solution.py:383
  600.5 2.9 copy.18
  (4 shorter events, 0.0 us)
Async XLA Ops:
  6.5 75.9 %reduce-scatter.5.cloned.1.call-start = ((), (), s32[]{:S(2)}) async-start(), calls=%async_computation.3 | async-start | bytes 4587520 | tf_op jit(solution)/shard_map/reduce_scatter | solution.py:411
  38.3 180.6 %reduce-scatter.3.cloned.1.call-start = ((), (), s32[]{:S(2)}) async-start(), calls=%async_computation.2 | async-start | bytes 8257536 | tf_op jit(solution)/shard_map/reduce_scatter | solution.py:411
  80.6 410.0 %all-gather.3.cloned.1.call-start = ((), (), s32[]{:S(2)}) async-start(), calls=%async_computation.4 | async-start | bytes 9175040 | tf_op jit(solution)/shard_map/all_gather | solution.py:433
Sparse Core Ops, SparseCore 0:
  38.4 43.9 reduce-scatter.4
  86.0 132.8 reduce-scatter.2
  220.5 69.5 all-gather.2
